TPU v7x, 256 devices: a whole 4x4x8 slice. The times are simulated.
256 devices in a mesh: row: 16 (over z, core), col: 16 (over x, y).
Axes of the slice: x: 4, y: 4, z: 8, core: 2. Of those that a mesh axis runs over, the one named last changes fastest.
Arguments:
- matrix: bfloat16 [7, 4096, 7, 4096], P(None, 'row', None, 'col'), may hold values from -1 to 3
- pivots: int32 [2, 256], replicated, may hold values from 256 to 28671, as said below
Outputs:
- factored: bfloat16 [7, 4096, 7, 4096], P(None, 'row', None, 'col')
Inputs may be any that keep to these rules, and one draw needn't show every extreme that they name: Within a step s the pivots[s, :] are distinct and lie in (s + 1) * 256 to 28671.
All inputs are finite; a program needn't handle non-finite values.
Results may differ from a plain program's by a relative error of at most 0.0059.
Values may be sent and summed in bfloat16 or wider, within the bound.
A program may use at most 64 MiB of HBM per device.

v0:
```python
import jax
import jax.numpy as jnp
from jax import lax
from jax.sharding import PartitionSpec as P

STEPS = 2
NEWTON = 3


def broadcast(shard, axis, root):
    mine = lax.axis_index(axis) == root
    return lax.psum(jnp.where(mine, shard, jnp.zeros_like(shard)), axis)


def newton_inverse(diag_block):
    identity = jnp.eye(diag_block.shape[0], dtype=jnp.float32)
    approx = identity / 3.0
    for _ in range(NEWTON):
        product = jnp.dot(diag_block, approx, precision=lax.Precision.HIGHEST)
        approx = jnp.dot(approx, 2.0 * identity - product, precision=lax.Precision.HIGHEST)
    return approx


def body(matrix, pivots):
    row_count = lax.axis_size("row")
    col_count = lax.axis_size("col")
    row_index = lax.axis_index("row")
    col_index = lax.axis_index("col")
    row_cycles, block_size, col_cycles, _ = matrix.shape
    local_rows = row_cycles * block_size
    local_cols = col_cycles * block_size
    current = matrix.reshape(local_rows, local_cols)
    row_positions = jnp.arange(local_rows, dtype=jnp.int32)
    col_positions = jnp.arange(local_cols, dtype=jnp.int32)
    global_row = (
        row_positions // block_size * row_count * block_size
        + row_index * block_size
        + row_positions % block_size
    )
    global_col = (
        col_positions // block_size * col_count * block_size
        + col_index * block_size
        + col_positions % block_size
    )
    identity = jnp.eye(block_size, dtype=jnp.float32)
    for panel_step in range(STEPS):
        after_row = (panel_step + 1) * block_size
        owner_row = panel_step % row_count
        owner_cycle = panel_step // row_count
        owner_col = panel_step % col_count
        panel_cycle = panel_step // col_count
        chosen = pivots[panel_step]
        owner_of = chosen // block_size % row_count
        local_at = chosen // (block_size * row_count) * block_size + chosen % block_size
        is_mine = owner_of == row_index
        picked = jnp.where(
            is_mine[:, None],
            current[jnp.clip(local_at, 0, local_rows - 1)],
            jnp.zeros((), jnp.bfloat16),
        )
        top_rows = current[owner_cycle * block_size : (owner_cycle + 1) * block_size]
        is_top = row_index == owner_row
        new_top = lax.psum(picked, "row").astype(jnp.float32).astype(jnp.bfloat16)
        old_top = broadcast(top_rows, "row", owner_row)
        target = jnp.where(is_mine, local_at, local_rows)
        current = current.at[target].set(old_top, mode="drop")
        kept_rows = current[owner_cycle * block_size : (owner_cycle + 1) * block_size]
        current = current.at[owner_cycle * block_size : (owner_cycle + 1) * block_size].set(
            jnp.where(is_top, new_top, kept_rows)
        )
        panel_block = current[:, panel_cycle * block_size : (panel_cycle + 1) * block_size]
        is_owner = col_index == owner_col
        diag_block = jnp.where(
            is_owner,
            new_top[:, panel_cycle * block_size : (panel_cycle + 1) * block_size].astype(
                jnp.float32
            ),
            3.0 * identity,
        )
        below_mask = (global_row >= after_row)[:, None]
        inverse = newton_inverse(diag_block)
        own_lower = jnp.where(
            below_mask,
            jnp.dot(panel_block.astype(jnp.float32), inverse, precision=lax.Precision.HIGHEST),
            0.0,
        ).astype(jnp.bfloat16)
        lower_panel = broadcast(own_lower, "col", owner_col)
        right_mask = (global_col >= after_row)[None, :]
        upper_rows = jnp.where(right_mask, new_top, jnp.zeros_like(new_top))
        change = jnp.dot(lower_panel, upper_rows, preferred_element_type=jnp.float32)
        current = (current.astype(jnp.float32) - change).astype(jnp.bfloat16)
        old_panel = current[:, panel_cycle * block_size : (panel_cycle + 1) * block_size]
        current = current.at[:, panel_cycle * block_size : (panel_cycle + 1) * block_size].set(
            jnp.where(jnp.logical_and(is_owner, below_mask), lower_panel, old_panel)
        )
    return current.reshape(row_cycles, block_size, col_cycles, block_size)


def solution(mesh):
    return jax.shard_map(
        body,
        mesh=mesh,
        in_specs=(P(None, "row", None, "col"), P()),
        out_specs=P(None, "row", None, "col"),
        check_vma=False,
    )
```

profile of v0, /device:TPU:32, one launch (start us, length us, event | category | flops | bytes accessed | tf_op | source)
XLA Modules:
  0.0 546.3 jit_solution(16321497234872604605)
XLA Ops:
  6.5 6.8 %copy.6 = bf16[7,256,7,256]{3,2,1,0:T(8,128)(2,1)S(1)} copy(bf16[7,256,7,256]{3,1,2,0:T(8,128)(2,1)} %param.10) | data formatting | bytes 12845056 | tf_op args[0]
  13.4 5.6 %copy.11 = bf16[224,8,7,256]{3,1,2,0:T(8,128)(2,1)} copy(bf16[224,8,7,256]{3,2,1,0:T(8,128)(2,1)S(1)} %bitcast.68) | data formatting | bytes 12845056
  19.0 0.6 copy.10
  19.7 1.4 copy.8
  21.2 5.8 %gather_fusion = bf16[256,1792]{1,0:T(8,128)(2,1)S(1)} fusion(bf16[1792,1792]{1,0:T(8,128)(2,1)} %bitcast.66, s32[1024]{0:T(1024)S(1)} %pad_clamp_fusion.1), kind=kCustom, calls=%fused_computation | custom fusion | bytes 1836032 | tf_op jit(solution)/shard_map/gather | solution.py:58
  27.0 1.1 broadcast_select_fusion.1
  28.1 0.5 all-reduce.7.cloned.1.call-start
  28.6 114.3 %all-reduce.13.cloned.1.call-done = (bf16[256,1792]{1,0:T(8,128)(2,1)}, bf16[256,1792]{1,0:T(8,128)(2,1)}) async-done(((bf16[256,1792]{1,0:T(8,128)(2,1)}, bf16[256,1792]{1,0:T(8,128)(2,1)}), (bf16[256,1792]{1,0:T(8,128)(2,1)}, bf16[256,1792]{1,0:T(8,128)(2,1)})) %all-reduce.13.cloned.1.call-update) | async-done | bytes 1835024 | tf_op jit(solution)/shard_map/psum | solution.py:12
  142.9 9.5 %scatter_fusion = bf16[1792,1792]{1,0:T(8,128)(2,1)} fusion(bf16[1792,1792]{1,0:T(8,128)(2,1)} %bitcast.67, s32[256]{0:T(256)S(1)} %bitcast.70, bf16[256,1792]{1,0:T(8,128)(2,1)} %get-tuple-element.55), kind=kCustom, calls=%fused_computation.2 | custom fusion | bytes 2753536 | tf_op jit(solution)/shard_map/scatter | solution.py:66
  152.4 2.3 fusion.9
  154.7 0.4 convolution_subtract_fusion.5
  155.5 0.4 convolution_subtract_fusion.4
  156.3 0.4 convolution_subtract_fusion.3
  157.1 3.1 fusion.3
  160.4 0.6 compare_reduce_fusion
  161.1 98.7 %all-reduce.7.cloned.1.call-done = bf16[1792,256]{1,0:T(8,128)(2,1)} async-done(((bf16[1792,256]{1,0:T(8,128)(2,1)}), bf16[1792,256]{1,0:T(8,128)(2,1)}) %all-reduce.7.cloned.1.call-update) | async-done | bytes 917520 | tf_op jit(solution)/shard_map/psum | solution.py:12
  259.9 7.8 %subtract_convert_fusion.1 = bf16[1792,1792]{1,0:T(8,128)(2,1)} fusion(bf16[1792,1792]{1,0:T(8,128)(2,1)} %fusion.9, bf16[1792,256]{1,0:T(8,128)(2,1)} %all-reduce.7.cloned.1.call-done, bf16[256,1792]{1,0:T(8,128)(2,1)S(1)} %copy-done.2, pred[1792]{0:T(1024)(128)(4,1)S(1)} %fusion.67), kind=kOutput, calls=%fused_computation.5 | convolution fusion | flops 1654259712 | bytes 14681856 | tf_op jit(solution)/shard_map/dot_general | solution.py:90
  267.6 3.3 fusion.4
  270.9 5.8 %gather_fusion.1 = bf16[256,1792]{1,0:T(8,128)(2,1)S(1)} fusion(bf16[1792,1792]{1,0:T(8,128)(2,1)} %fusion.4, s32[1024]{0:T(1024)S(1)} %pad_clamp_fusion), kind=kCustom, calls=%fused_computation.1 | custom fusion | bytes 1836032 | tf_op jit(solution)/shard_map/gather | solution.py:58
  276.7 2.6 slice_select_fusion.1
  279.5 111.2 %all-reduce.11.cloned.1.call-done = (bf16[256,1792]{1,0:T(8,128)(2,1)}, bf16[256,1792]{1,0:T(8,128)(2,1)}) async-done(((bf16[256,1792]{1,0:T(8,128)(2,1)}, bf16[256,1792]{1,0:T(8,128)(2,1)}), (bf16[256,1792]{1,0:T(8,128)(2,1)}, bf16[256,1792]{1,0:T(8,128)(2,1)})) %all-reduce.11.cloned.1.call-update) | async-done | bytes 1835024 | tf_op jit(solution)/shard_map/psum | solution.py:12
  390.7 9.7 %scatter_fusion.1 = bf16[1792,1792]{1,0:T(8,128)(2,1)} fusion(bf16[1792,1792]{1,0:T(8,128)(2,1)} %fusion.4, s32[256]{0:T(256)S(1)} %bitcast.71, bf16[256,1792]{1,0:T(8,128)(2,1)} %get-tuple-element.53), kind=kCustom, calls=%fused_computation.3 | custom fusion | bytes 2753536 | tf_op jit(solution)/shard_map/scatter | solution.py:66
  400.4 2.3 fusion.7
  402.7 0.4 convolution_subtract_fusion.2
  403.5 0.4 convolution_subtract_fusion.1
  404.3 0.4 convolution_subtract_fusion
  405.1 3.1 fusion.2
  408.2 99.6 %all-reduce.9.cloned.1.call-done = bf16[1792,256]{1,0:T(8,128)(2,1)} async-done(((bf16[1792,256]{1,0:T(8,128)(2,1)}), bf16[1792,256]{1,0:T(8,128)(2,1)}) %all-reduce.9.cloned.1.call-update) | async-done | bytes 917520 | tf_op jit(solution)/shard_map/psum | solution.py:12
  507.9 7.8 %subtract_convert_fusion = bf16[1792,1792]{1,0:T(8,128)(2,1)} fusion(bf16[1792,1792]{1,0:T(8,128)(2,1)} %fusion.7, bf16[1792,256]{1,0:T(8,128)(2,1)} %all-reduce.9.cloned.1.call-done, bf16[256,1792]{1,0:T(8,128)(2,1)S(1)} %copy-done.3, pred[1792]{0:T(1024)(128)(4,1)S(1)} %fusion.66), kind=kOutput, calls=%fused_computation.4 | convolution fusion | flops 1654259712 | bytes 14681856 | tf_op jit(solution)/shard_map/dot_general | solution.py:90
  515.6 3.3 fusion.5
  518.9 13.0 %reshape.600 = bf16[7,256,7,256]{3,2,1,0:T(8,128)(2,1)} reshape(bf16[1792,1792]{1,0:T(8,128)(2,1)} %fusion.5) | data formatting | bytes 12845056 | tf_op jit(solution)/shard_map/reshape | solution.py:96
  532.0 7.6 %copy.9 = bf16[7,256,7,256]{3,1,2,0:T(8,128)(2,1)} copy(bf16[7,256,7,256]{3,2,1,0:T(8,128)(2,1)} %reshape.600) | data formatting | bytes 12845056 | tf_op jit(solution)/shard_map/reshape | solution.py:96
  (40 shorter events, 2.9 us)
Async XLA Ops:
  6.5 136.4 %all-reduce.13.cloned.1.call-start = ((), (), s32[]{:S(2)}) async-start(), calls=%async_computation.3 | async-start | bytes 3670016 | tf_op jit(solution)/shard_map/psum | solution.py:12
  6.5 6.8 %copy-start.4 = (s32[2,256]{1,0:T(2,128)S(1)}, s32[2,256]{1,0:T(2,128)}, u32[]{:S(2)}) copy-start(s32[2,256]{1,0:T(2,128)} %param.11) | copy-start | bytes 6148
  13.4 5.6 %slice-start = ((bf16[7,256,7,256]{3,1,2,0:T(8,128)(2,1)}), bf16[1,256,7,256]{3,1,2,0:T(8,128)(2,1)S(1)}, s32[]{:S(2)}) async-start(bf16[7,256,7,256]{3,1,2,0:T(8,128)(2,1)} %param.10), calls=%async_computation.4 | async-start | bytes 1835008 | tf_op jit(solution)/shard_map/slice | solution.py:61
  28.1 231.8 %all-reduce.7.cloned.1.call-start = ((), (), s32[]{:S(2)}) async-start(), calls=%async_computation | async-start | bytes 1835008 | tf_op jit(solution)/shard_map/psum | solution.py:12
  142.9 9.5 %copy-start.2 = (bf16[256,1792]{1,0:T(8,128)(2,1)S(1)}, bf16[256,1792]{1,0:T(8,128)(2,1)}, u32[]{:S(2)}) copy-start(bf16[256,1792]{1,0:T(8,128)(2,1)} %get-tuple-element.56) | copy-start | bytes 2752516
  160.2 230.5 %all-reduce.11.cloned.1.call-start = ((), (), s32[]{:S(2)}) async-start(), calls=%async_computation.2 | async-start | bytes 3670016 | tf_op jit(solution)/shard_map/psum | solution.py:12
  259.9 7.8 %copy-start = (bf16[1792,256]{1,0:T(8,128)(2,1)S(1)}, bf16[1792,256]{1,0:T(8,128)(2,1)}, u32[]{:S(2)}) copy-start(bf16[1792,256]{1,0:T(8,128)(2,1)} %all-reduce.7.cloned.1.call-done) | copy-start | bytes 2752516
  279.4 228.5 %all-reduce.9.cloned.1.call-start = ((), (), s32[]{:S(2)}) async-start(), calls=%async_computation.1 | async-start | bytes 1835008 | tf_op jit(solution)/shard_map/psum | solution.py:12
  390.7 9.7 %copy-start.3 = (bf16[256,1792]{1,0:T(8,128)(2,1)S(1)}, bf16[256,1792]{1,0:T(8,128)(2,1)}, u32[]{:S(2)}) copy-start(bf16[256,1792]{1,0:T(8,128)(2,1)} %get-tuple-element.54) | copy-start | bytes 2752516
  507.9 7.8 %copy-start.1 = (bf16[1792,256]{1,0:T(8,128)(2,1)S(1)}, bf16[1792,256]{1,0:T(8,128)(2,1)}, u32[]{:S(2)}) copy-start(bf16[1792,256]{1,0:T(8,128)(2,1)} %all-reduce.9.cloned.1.call-done) | copy-start | bytes 2752516
Sparse Core Ops, SparseCore 0:
  28.2 114.6 all-reduce.12
  160.3 99.4 all-reduce.6
  279.5 111.1 all-reduce.10
  408.3 99.4 all-reduce.8
where the time goes:
time: 555 us; the launch traced here: 546 us
  waiting for transfers between devices  424 us (76%)
  local copies, waits for them, and re-layouts  65.8 us (12%)
  matrix products  26.3 us (5%)
  other arithmetic  15.8 us (3%)
  between operations  13.6 us (2%)
    psum x4, waiting for transfers between devices, broadcast(): return lax.psum(jnp.where(mine, shard, jnp.zeros_like(shard)), axis)  424 us
    reshape x2, local copies, waits for them, and re-layouts, body(): return current.reshape(row_cycles, block_size, col_cycles, block_size)  20.6 us
    scatter x2, local copies, waits for them, and re-layouts, body(): current = current.at[target].set(old_top, mode='drop')  19.2 us
    dot_general x2, matrix products, body(): jnp.dot(lower_panel, upper_rows, preferred_element_type=jnp.float32)  15.6 us
    unnamed x13, local copies, waits for them, and re-layouts  13 us
    gather x2, local copies, waits for them, and re-layouts, body(): current[jnp.clip(local_at, 0, local_rows - 1)]  11.6 us
  transfers between devices with their start and end apart: 4, of which 4 were waited for; matrix products, arithmetic and copies ran while one was open for 0% of the time, Pallas kernels for 0%

commit v1 on v0

--- a/solution.py
+++ b/solution.py
@@ -9,7 +9,7 @@
 
 def broadcast(shard, axis, root):
     mine = lax.axis_index(axis) == root
-    return lax.psum(jnp.where(mine, shard, jnp.zeros_like(shard)), axis)
+    return jnp.sum(lax.all_gather(jnp.where(mine, shard, jnp.zeros_like(shard)), axis_name=axis), 0)
 
 
 def newton_inverse(diag_block):

time: 555 us -> 763 us (1.37)
  waiting for transfers between devices: 424 us -> 594 us
  other arithmetic: 15.8 us -> 48.1 us
    all_gather x0 -> x4, waiting for transfers between devices: none -> 378 us  [broadcast(): lax.all_gather(jnp.where(mine, shard, jnp.zeros_like(shard)), axis_name=a...]
    psum x4 -> x2, waiting for transfers between devices: 424 us -> 216 us  [body(): new_top = lax.psum(picked, 'row').astype(jnp.float32).astype(jnp.bfloat16)]
    reduce_sum x0 -> x4, other arithmetic: none -> 31 us  [broadcast(): jnp.sum(lax.all_gather(jnp.where(mine, shard, jnp.zeros_like(shard)), axi...]
  transfers between devices with their start and end apart: 4 -> 6, of which waited for: 4 -> 6; matrix products, arithmetic and copies ran while one was open for 0% -> 2% of each run, Pallas kernels for 0% -> 0%
where the time goes in v1:
time: 763 us; the launch traced here: 753 us
  waiting for transfers between devices  594 us (78%)
  local copies, waits for them, and re-layouts  65.3 us (9%)
  other arithmetic  48.1 us (6%)
  matrix products  30.9 us (4%)
  between operations  13.9 us (2%)
    all_gather x4, waiting for transfers between devices, broadcast(): lax.all_gather(jnp.where(mine, shard, jnp.zeros_like(shard)), axis_name=a...  378 us
    psum x2, waiting for transfers between devices, body(): new_top = lax.psum(picked, 'row').astype(jnp.float32).astype(jnp.bfloat16)  216 us
    reduce_sum x4, other arithmetic, broadcast(): jnp.sum(lax.all_gather(jnp.where(mine, shard, jnp.zeros_like(shard)), axi...  31 us
    reshape x2, local copies, waits for them, and re-layouts, body(): return current.reshape(row_cycles, block_size, col_cycles, block_size)  20.6 us
    scatter x2, local copies, waits for them, and re-layouts, body(): current = current.at[target].set(old_top, mode='drop')  17.9 us
  transfers between devices with their start and end apart: 6, of which 6 were waited for; matrix products, arithmetic and copies ran while one was open for 2% of the time, Pallas kernels for 0%

profile of v1, /device:TPU:32, one launch (start us, length us, event | category | flops | bytes accessed | tf_op | source)
XLA Modules:
  0.0 753.0 jit_solution(10205768175777310580)
XLA Ops:
  8.0 6.8 copy.8
  14.8 5.6 copy.16
  20.5 5.9 gather_fusion
  28.2 1.4 copy.10
  29.9 109.4 %all-reduce.3.cloned.1.call-done = bf16[256,1792]{1,0:T(8,128)(2,1)} async-done(((bf16[256,1792]{1,0:T(8,128)(2,1)}), bf16[256,1792]{1,0:T(8,128)(2,1)}) %all-reduce.3.cloned.1.call-update) | async-done | bytes 917520 | tf_op jit(solution)/shard_map/psum | solution.py:63
  141.0 1.3 convolution_subtract_fusion.4
  142.7 1.3 convolution_subtract_fusion.3
  144.4 83.4 %all-gather.8.cloned.1.call-done = bf16[16,256,1792]{2,1,0:T(8,128)(2,1)} async-done(((bf16[1,256,1792]{2,1,0:T(8,128)(2,1)}), bf16[16,256,1792]{2,1,0:T(8,128)(2,1)}) %all-gather.8.cloned.1.call-update) | async-done | bytes 14680080 | tf_op jit(solution)/shard_map/all_gather | solution.py:12
  227.8 7.7 %reduce_sum.48 = bf16[256,1792]{1,0:T(8,128)(2,1)S(1)} reduce(bf16[16,256,1792]{2,1,0:T(8,128)(2,1)} %all-gather.8.cloned.1.call-done, bf16[]{:T(256)} %constant.238.clone.1), dimensions={0}, to_apply=%region_0.1 | reduce | flops 6881280 | bytes 15597570 | tf_op jit(solution)/shard_map/reduce_sum | solution.py:12
  235.6 8.9 %scatter_fusion = bf16[1792,1792]{1,0:T(8,128)(2,1)} fusion(bf16[1792,1792]{1,0:T(8,128)(2,1)} %bitcast.70, s32[256]{0:T(256)S(1)} %bitcast.76, bf16[256,1792]{1,0:T(8,128)(2,1)S(1)} %reduce_sum.48), kind=kCustom, calls=%fused_computation.2 | custom fusion | bytes 2753536 | tf_op jit(solution)/shard_map/scatter | solution.py:66
  244.5 2.3 fusion.9
  246.8 3.0 fusion.3
  250.8 105.1 %all-gather.10.cloned.1.call-done = bf16[28672,256]{1,0:T(8,128)(2,1)} async-done(((bf16[1792,256]{1,0:T(8,128)(2,1)}), bf16[28672,256]{1,0:T(8,128)(2,1)}) %all-gather.10.cloned.1.call-update) | async-done | bytes 14680080 | tf_op jit(solution)/shard_map/all_gather | solution.py:12
  355.9 7.8 %reduce_sum.49 = bf16[1792,256]{1,0:T(8,128)(2,1)S(1)} reduce(bf16[16,1792,256]{2,1,0:T(8,128)(2,1)} %bitcast.73, bf16[]{:T(256)} %constant.238.clone.1), dimensions={0}, to_apply=%region_3.4 | reduce | flops 6881280 | bytes 15597570 | tf_op jit(solution)/shard_map/reduce_sum | solution.py:12
  363.7 7.4 subtract_convert_fusion.1
  371.1 3.3 fusion.4
  374.4 5.8 gather_fusion.1
  381.4 2.2 slice_select_fusion.1
  384.0 106.3 %all-reduce.5.cloned.1.call-done = bf16[256,1792]{1,0:T(8,128)(2,1)} async-done(((bf16[256,1792]{1,0:T(8,128)(2,1)}), bf16[256,1792]{1,0:T(8,128)(2,1)}) %all-reduce.5.cloned.1.call-update) | async-done | bytes 917520 | tf_op jit(solution)/shard_map/psum | solution.py:63
  492.0 1.3 convolution_subtract_fusion.1
  493.7 1.3 convolution_subtract_fusion
  495.4 83.3 %all-gather.12.cloned.1.call-done = bf16[4096,1792]{1,0:T(8,128)(2,1)} async-done(((bf16[256,1792]{1,0:T(8,128)(2,1)}), bf16[4096,1792]{1,0:T(8,128)(2,1)}) %all-gather.12.cloned.1.call-update) | async-done | bytes 14680080 | tf_op jit(solution)/shard_map/all_gather | solution.py:12
  578.7 7.7 %reduce_sum.50 = bf16[256,1792]{1,0:T(8,128)(2,1)S(1)} reduce(bf16[16,256,1792]{2,1,0:T(8,128)(2,1)} %bitcast.72, bf16[]{:T(256)} %constant.238.clone.1), dimensions={0}, to_apply=%region_5.6 | reduce | flops 6881280 | bytes 15597570 | tf_op jit(solution)/shard_map/reduce_sum | solution.py:12
  586.4 9.0 %scatter_fusion.1 = bf16[1792,1792]{1,0:T(8,128)(2,1)} fusion(bf16[1792,1792]{1,0:T(8,128)(2,1)} %fusion.4, s32[256]{0:T(256)S(1)} %bitcast.77, bf16[256,1792]{1,0:T(8,128)(2,1)S(1)} %reduce_sum.50), kind=kCustom, calls=%fused_computation.3 | custom fusion | bytes 2753536 | tf_op jit(solution)/shard_map/scatter | solution.py:66
  595.4 2.3 fusion.7
  597.7 3.0 fusion.2
  600.8 106.0 %all-gather.14.cloned.1.call-done = bf16[28672,256]{1,0:T(8,128)(2,1)} async-done(((bf16[1792,256]{1,0:T(8,128)(2,1)}), bf16[28672,256]{1,0:T(8,128)(2,1)}) %all-gather.14.cloned.1.call-update) | async-done | bytes 14680080 | tf_op jit(solution)/shard_map/all_gather | solution.py:12
  706.9 7.8 %reduce_sum.51 = bf16[1792,256]{1,0:T(8,128)(2,1)S(1)} reduce(bf16[16,1792,256]{2,1,0:T(8,128)(2,1)} %bitcast.74, bf16[]{:T(256)} %constant.238.clone.1), dimensions={0}, to_apply=%region_8.9 | reduce | flops 6881280 | bytes 15597570 | tf_op jit(solution)/shard_map/reduce_sum | solution.py:12
  714.7 7.4 subtract_convert_fusion
  722.1 3.3 fusion.5
  725.4 13.0 %reshape.610 = bf16[7,256,7,256]{3,2,1,0:T(8,128)(2,1)} reshape(bf16[1792,1792]{1,0:T(8,128)(2,1)} %fusion.5) | data formatting | bytes 12845056 | tf_op jit(solution)/shard_map/reshape | solution.py:96
  738.4 7.6 %copy.13 = bf16[7,256,7,256]{3,1,2,0:T(8,128)(2,1)} copy(bf16[7,256,7,256]{3,2,1,0:T(8,128)(2,1)} %reshape.610) | data formatting | bytes 12845056 | tf_op jit(solution)/shard_map/reshape | solution.py:96
  (47 shorter events, 11.1 us)
Async XLA Ops:
  6.5 132.8 %all-reduce.3.cloned.1.call-start = ((), (), s32[]{:S(2)}) async-start(), calls=%async_computation.1 | async-start | bytes 1835008 | tf_op jit(solution)/shard_map/psum | solution.py:63
  14.8 5.6 copy-start.2
  20.5 7.1 slice-start
  27.5 200.4 %all-gather.8.cloned.1.call-start = ((), (), s32[]{:S(2)}) async-start(), calls=%async_computation | async-start | bytes 15597568 | tf_op jit(solution)/shard_map/all_gather | solution.py:12
  29.7 326.2 %all-gather.10.cloned.1.call-start = ((), (), s32[]{:S(2)}) async-start(), calls=%async_computation.3 | async-start | bytes 15597568 | tf_op jit(solution)/shard_map/all_gather | solution.py:12
  235.6 8.9 %copy-start = (bf16[256,1792]{1,0:T(8,128)(2,1)S(1)}, bf16[256,1792]{1,0:T(8,128)(2,1)}, u32[]{:S(2)}) copy-start(bf16[256,1792]{1,0:T(8,128)(2,1)} %all-reduce.3.cloned.1.call-done) | copy-start | bytes 2752516
  249.8 240.5 %all-reduce.5.cloned.1.call-start = ((), (), s32[]{:S(2)}) async-start(), calls=%async_computation.2 | async-start | bytes 1835008 | tf_op jit(solution)/shard_map/psum | solution.py:63
  381.3 197.3 %all-gather.12.cloned.1.call-start = ((), (), s32[]{:S(2)}) async-start(), calls=%async_computation.4 | async-start | bytes 15597568 | tf_op jit(solution)/shard_map/all_gather | solution.py:12
  383.6 323.3 %all-gather.14.cloned.1.call-start = ((), (), s32[]{:S(2)}) async-start(), calls=%async_computation.5 | async-start | bytes 15597568 | tf_op jit(solution)/shard_map/all_gather | solution.py:12
  586.4 9.0 %copy-start.1 = (bf16[256,1792]{1,0:T(8,128)(2,1)S(1)}, bf16[256,1792]{1,0:T(8,128)(2,1)}, u32[]{:S(2)}) copy-start(bf16[256,1792]{1,0:T(8,128)(2,1)} %all-reduce.5.cloned.1.call-done) | copy-start | bytes 2752516
Sparse Core Ops, SparseCore 0:
  27.6 111.6 all-reduce.2
  141.2 86.6 all-gather.7
  249.9 105.9 all-gather.9
  381.4 108.8 all-reduce.4
  492.0 86.6 all-gather.11
  600.9 105.9 all-gather.13
